TPU v7x, 256 devices: a whole 4x4x8 slice. The times are simulated.
256 devices in a mesh: dp: 32 (over z, y), ctx: 8 (over x, core).
Axes of the slice: x: 4, y: 4, z: 8, core: 2. Of those that a mesh axis runs over, the one named last changes fastest.
Arguments:
- query_rows: bfloat16 [32768, 4096], P(('dp', 'ctx')), may hold values from -9 to 9
- key_rows: bfloat16 [32768, 1024], P(('dp', 'ctx')), may hold values from -4 to 4
- token_values: bfloat16 [32768, 1024], P(('dp', 'ctx')), may hold values from -6 to 6
- group_of_row: int32 [32768, 1], P(('dp', 'ctx')), may hold values from 0 to 31; in each aligned block of 128 rows (0 to 127, 128 to 255, ...) at most 8 rows name the same one
- doc_lengths: int32 [32, 2], P('dp'), may hold values from 1 to 1536, 2048 in all within a row
Outputs:
- attended: bfloat16 [32768, 4096], P(('dp', 'ctx'))
Inputs may be any that keep to these rules, and one draw needn't show every extreme that they name: `group_of_row`: within each device's block of 128 rows no group is named by more than 8 rows; in some blocks one group is named by exactly 8. `doc_lengths`: each group's 2 lengths sum to 2048; neither exceeds 1536.
All inputs are finite; a program needn't handle non-finite values.
Results may differ from a plain program's by a relative error of at most 0.0038.
Values may be sent and summed in bfloat16 or wider, within the bound.
No kernel may reach another device: no remote copies, remote signals or barrier semaphores. Data moves between devices by JAX's collectives and lax.ppermute only.
A program may use at most 128 MiB of HBM per device.

v0:
```python
import math
import jax
import jax.numpy as jnp
from jax import lax
from jax.sharding import PartitionSpec as P

QUERY_HEAD_COUNT = 32
KEY_VALUE_HEADS = 8
HEAD_SIZE = 128
masked_score = -1e30


def rank_rows(indices):
    count_all = indices.shape[0]
    rows_per_block = 128
    usable = indices >= 0

    def count_before(pieces):
        earlier = usable[None, :] & (indices[None, :] < pieces[:, None])
        return jnp.sum(earlier.astype(jnp.int32), axis=1)

    counted = lax.map(count_before, indices.reshape(count_all // rows_per_block, rows_per_block))
    return counted.reshape(count_all)


def document_ids(ranks, starts):
    return jnp.sum((starts[None, :] <= ranks[:, None]).astype(jnp.int32), axis=1) - 1


def attend(block_of_queries, key_heads, value_heads, query_index, query_doc, key_index, key_doc):
    head_dim = key_heads.shape[2]
    scores = jnp.einsum(
        "qjgd,kjd->jgqk", block_of_queries, key_heads, preferred_element_type=jnp.float32
    )
    scores = scores * (1.0 / math.sqrt(head_dim))
    allowed = (
        (query_doc[:, None] == key_doc[None, :])
        & (key_index[None, :] <= query_index[:, None])
        & (key_index[None, :] >= 0)
    )
    scores = jnp.where(allowed[None, None], scores, masked_score)
    row_max = jnp.max(scores, axis=3, keepdims=True)
    weights = jnp.exp(scores - row_max)
    totals = jnp.sum(weights, axis=3)
    output = jnp.einsum(
        "jgqk,kjd->qjgd",
        weights.astype(jnp.bfloat16),
        value_heads,
        preferred_element_type=jnp.float32,
    )
    output = output / jnp.transpose(totals, (2, 0, 1))[..., None]
    return output.reshape(
        output.shape[0], output.shape[1], output.shape[2] * output.shape[3]
    ).astype(jnp.bfloat16)


def attend_all(query_heads, query_index, query_doc, key_heads, value_heads, key_index, key_doc):
    count_q = query_heads.shape[0]
    rows_per_block = min(128, count_q)
    blocks = count_q // rows_per_block

    def one_block(inputs_block):
        return attend(
            inputs_block[0],
            key_heads,
            value_heads,
            inputs_block[1],
            inputs_block[2],
            key_index,
            key_doc,
        )

    shaped = (
        query_heads.reshape((blocks, rows_per_block) + query_heads.shape[1:]),
        query_index.reshape(blocks, rows_per_block),
        query_doc.reshape(blocks, rows_per_block),
    )
    result = lax.map(one_block, shaped)
    return result.reshape((count_q,) + result.shape[2:])


def body(query_rows, key_rows, token_values, group_of_row, doc_lengths):
    dp_count = lax.axis_size("dp")
    tok_rows = query_rows.shape[0]
    slot_rows = 2 * tok_rows // dp_count
    key_value_head_count = KEY_VALUE_HEADS
    head_dim = HEAD_SIZE
    rows_per_group = QUERY_HEAD_COUNT // KEY_VALUE_HEADS
    group_ids = group_of_row[:, 0]
    onehot = (group_ids[:, None] == jnp.arange(dp_count, dtype=jnp.int32)[None, :]).astype(
        jnp.int32
    )
    position = jnp.sum((jnp.cumsum(onehot, axis=0) - onehot) * onehot, axis=1)
    target = group_ids * slot_rows + position
    stream = lax.axis_index(("dp", "ctx")) * tok_rows + jnp.arange(tok_rows, dtype=jnp.int32)
    send_count = dp_count * slot_rows
    send_query = (
        jnp.zeros((send_count, query_rows.shape[1]), jnp.bfloat16).at[target].set(query_rows)
    )
    send_key = jnp.zeros((send_count, key_rows.shape[1]), jnp.bfloat16).at[target].set(key_rows)
    send_value = (
        jnp.zeros((send_count, token_values.shape[1]), jnp.bfloat16).at[target].set(token_values)
    )
    send_index = jnp.full((send_count,), -1, jnp.int32).at[target].set(stream)
    arrived = (
        lax.all_to_all(
            send_query.reshape(dp_count, slot_rows, query_rows.shape[1]),
            "dp",
            split_axis=0,
            concat_axis=0,
            tiled=True,
        ),
        lax.all_to_all(
            send_key.reshape(dp_count, slot_rows, key_rows.shape[1]),
            "dp",
            split_axis=0,
            concat_axis=0,
            tiled=True,
        ),
        lax.all_to_all(
            send_value.reshape(dp_count, slot_rows, token_values.shape[1]),
            "dp",
            split_axis=0,
            concat_axis=0,
            tiled=True,
        ),
        lax.all_to_all(
            send_index.reshape(dp_count, slot_rows), "dp", split_axis=0, concat_axis=0, tiled=True
        ),
    )
    local_query = arrived[0].reshape(send_count, key_value_head_count, rows_per_group * head_dim)
    local_key = arrived[1].reshape(send_count, key_value_head_count, head_dim)
    local_value = arrived[2].reshape(send_count, key_value_head_count, head_dim)
    local_index = arrived[3].reshape(send_count)
    lengths = doc_lengths[0]
    starts = jnp.cumsum(lengths) - lengths
    group_key, group_value, group_index = (
        lax.all_gather(local_key, "ctx", axis=0, tiled=True),
        lax.all_gather(local_value, "ctx", axis=0, tiled=True),
        lax.all_gather(local_index, "ctx", axis=0, tiled=True),
    )
    group_doc = document_ids(rank_rows(group_index), starts)
    own_doc = lax.dynamic_slice_in_dim(group_doc, lax.axis_index("ctx") * send_count, send_count, 0)
    result = attend_all(
        local_query.reshape(send_count, key_value_head_count, rows_per_group, head_dim),
        local_index,
        own_doc,
        group_key,
        group_value,
        group_index,
        group_doc,
    )
    back_rows = result.reshape(send_count, key_value_head_count * rows_per_group * head_dim)
    returned = lax.all_to_all(
        back_rows.reshape(dp_count, slot_rows, back_rows.shape[1]),
        "dp",
        split_axis=0,
        concat_axis=0,
        tiled=True,
    )
    return returned.reshape(send_count, back_rows.shape[1])[target]


def solution(mesh):
    in_specs = (
        P(("dp", "ctx"), None),
        P(("dp", "ctx"), None),
        P(("dp", "ctx"), None),
        P(("dp", "ctx"), None),
        P("dp", None),
    )
    out_specs = P(("dp", "ctx"), None)
    return jax.shard_map(body, mesh=mesh, in_specs=in_specs, out_specs=out_specs, check_vma=False)
```

profile of v0, /device:TPU:8, one launch (start us, length us, event | category | flops | bytes accessed | tf_op | source)
XLA Modules:
  0.0 317.4 jit_solution(16999272624418811626)
XLA Ops:
  6.5 0.7 fusion.24
  7.5 0.8 select_reduce_fusion
  8.3 0.7 fusion.26
  9.0 1.7 scatter_custom_fusion.2
  10.7 28.3 %all_to_all.29 = bf16[32,8,1024]{2,1,0:T(8,128)(2,1)S(1)} all-to-all(bf16[32,8,1024]{2,1,0:T(8,128)(2,1)S(1)} %bitcast.108), channel_id=1, replica_groups=mesh['dp'=32,'ctx'=8] {'dp'}, dimensions={0} | all-to-all | bytes 1048576 | tf_op jit(solution)/shard_map/all_to_all | solution.py:113
  39.0 0.9 copy.26
  40.0 1.7 scatter_custom_fusion.3
  41.7 21.3 %all_to_all.30 = bf16[32,8,1024]{2,1,0:T(8,128)(2,1)S(1)} all-to-all(bf16[32,8,1024]{2,1,0:T(8,128)(2,1)S(1)} %bitcast.109), channel_id=1, replica_groups=mesh['dp'=32,'ctx'=8] {'dp'}, dimensions={0} | all-to-all | bytes 1048576 | tf_op jit(solution)/shard_map/all_to_all | solution.py:120
  63.1 0.9 copy.27
  64.0 1.0 scatter_custom_fusion
  65.0 0.7 all_to_all.18
  65.7 5.6 %all-to-all-start = ((s32[32,1,8]{2,1,0:T(1,128)}), s32[32,1,8]{2,1,0:T(1,128)S(1)}, u32[]{:S(2)}, u32[]{:S(2)}) async-start(s32[32,1,8]{2,1,0:T(1,128)} %bitcast.17), calls=%async_computation | async-start | bytes 32768 | tf_op jit(solution)/shard_map/all_to_all | solution.py:127
  71.5 4.4 %scatter_custom_fusion.1 = bf16[256,4096]{1,0:T(8,128)(2,1)} fusion(s32[128]{0:T(128)S(1)} %fusion.26, bf16[128,4096]{1,0:T(8,128)(2,1)} %param.9, bf16[]{:T(256)} %constant.33.clone.1), kind=kCustom, calls=%fused_computation.31 | custom fusion | bytes 2097664 | tf_op jit(solution)/shard_map/scatter | solution.py:98
  75.8 4.0 %all-to-all-done = s32[32,1,8]{2,1,0:T(1,128)S(1)} async-done(((s32[32,1,8]{2,1,0:T(1,128)}), s32[32,1,8]{2,1,0:T(1,128)S(1)}, u32[]{:S(2)}, u32[]{:S(2)}) %all-to-all-start) | async-done | bytes 1056 | tf_op jit(solution)/shard_map/all_to_all | solution.py:127
  79.8 5.8 %all-to-all-start.1 = ((bf16[32,8,4096]{2,1,0:T(8,128)(2,1)}), bf16[32,8,4096]{2,1,0:T(8,128)(2,1)S(1)}, u32[]{:S(2)}, u32[]{:S(2)}) async-start(bf16[32,8,4096]{2,1,0:T(8,128)(2,1)} %bitcast.22), calls=%async_computation.1 | async-start | bytes 4194304 | tf_op jit(solution)/shard_map/all_to_all | solution.py:106
  85.6 0.5 broadcast.116
  86.2 0.7 reduce.5
  87.0 11.0 %all-gather = s32[8,1,256]{2,1,0:T(1,128)S(1)} all-gather(s32[1,1,256]{2,1,0:T(1,128)S(1)} %reshape.188), channel_id=1, replica_groups=mesh['dp'=32,'ctx'=8] {'ctx'}, dimensions={0}, use_global_device_ids=true | all-gather | bytes 9216 | tf_op jit(solution)/shard_map/all_gather | solution.py:140
  98.1 5.6 %while.20 = (s32[]{:T(128)}, s32[16,128]{1,0:T(8,128)S(1)}, pred[2048]{0:T(1024)(128)(4,1)S(1)}, s32[2048]{0:T(1024)S(1)}, s32[16,128]{1,0:T(8,128)S(1)}, /*index=5*/s32[]{:T(128)}, s32[]{:T(128)}) while((s32[]{:T(128)}, s32[16,128]{1,0:T(8,128)S(1)}, pred[2048]{0:T(1024)(128)(4,1)S(1)}, s32[2048]{0:T(1024)S(1)}, s32[16,128]{1,0:T(8,128)S(1)}, ...), condition=%wide.region_7.8_spmd, body=%wide.region_5.7_spmd.sunk | while | flops 1048450 | bytes 13397 | solution.py:22
  98.1 0.3 convert_reduce_fusion.2
  98.4 0.3 convert_reduce_fusion.2
  98.8 0.3 convert_reduce_fusion.2
  99.1 0.3 convert_reduce_fusion.2
  99.5 0.3 convert_reduce_fusion.2
  99.8 0.3 convert_reduce_fusion.2
  103.8 30.9 %all-to-all-done.1 = bf16[32,8,4096]{2,1,0:T(8,128)(2,1)S(1)} async-done(((bf16[32,8,4096]{2,1,0:T(8,128)(2,1)}), bf16[32,8,4096]{2,1,0:T(8,128)(2,1)S(1)}, u32[]{:S(2)}, u32[]{:S(2)}) %all-to-all-start.1) | async-done | bytes 2097184 | tf_op jit(solution)/shard_map/all_to_all | solution.py:106
  134.8 2.7 reshape_reshape_reshape.6
  137.5 4.8 %copy.18 = bf16[2048,8,128]{2,0,1:T(8,128)(2,1)} copy(bf16[2048,8,128]{2,1,0:T(8,128)(2,1)} %all-gather.4.cloned.1.call-done) | data formatting | bytes 8388608 | tf_op jit(solution)/shard_map/while | solution.py:78
  142.2 6.7 %copy.19 = bf16[2048,8,128]{0,2,1:T(8,128)(2,1)} copy(bf16[2048,8,128]{2,1,0:T(8,128)(2,1)} %all-gather.6.cloned.1.call-done) | data formatting | bytes 8388608 | tf_op jit(solution)/shard_map/while | solution.py:78
  148.9 102.2 %while.21 = (s32[]{:T(128)}, bf16[2,128,8,512]{3,2,1,0:T(8,128)(2,1)}, s32[2,128]{1,0:T(2,128)S(1)}, s32[2048]{0:T(1024)S(1)}, s32[2048]{0:T(1024)S(1)}, /*index...) while((s32[]{:T(128)}, ...), condition=%wide.region_14.15_spmd, body=%wide.region_11.14_spmd.sunk | while | flops 4389332992 | bytes 118603368 | solution.py:78
  148.9 0.3 and_and_fusion.2
  149.3 1.6 constant_dynamic-slice_fusion.4
  150.9 16.3 %bitcast_reduce_fusion.2 = (f32[8,4,128]{2,1,0:T(4,128)S(1)}, f32[8,128,4,2048]{3,1,2,0:T(8,128)}) fusion(pred[128,2048]{1,0:T(8,128)(4,1)S(1)} %and_and_fusion.2, bf16[2048,8,128]{2,0,1:T(8,128)(2,1)} %get-tuple-element.282, bf16[1,128,8,4,128]{4,3,2,1,0:T(4,128)(2,1)S(1)} %constant_dynamic-slice_fusion.4), kind=kOutput, calls=%fused_computation.8.clone.1 | convolution fusion | flops 2172645376 | bytes 39075840 | tf_op jit(solution)/shard_map/while/body/eval_jaxpr/qjgd,kjd->jgqk/dot_general | solution.py:32
  167.1 15.0 %fusion.37 = f32[8,4,128]{2,1,0:T(4,128)S(1)} fusion(f32[8,128,4,2048]{3,1,2,0:T(8,128)} %get-tuple-element.232, f32[8,4,128]{2,1,0:T(4,128)S(1)} %get-tuple-element.233, pred[128,2048]{1,0:T(8,128)(4,1)S(1)} %and_and_fusion.2), kind=kLoop, calls=%fused_computation.11.clone.1 | loop fusion | flops 33550336 | bytes 33849344 | tf_op jit(solution)/shard_map/while/body/eval_jaxpr/reduce_sum | solution.py:44
  182.1 15.9 %fusion.38 = bf16[128,8,4,128]{0,3,2,1:T(8,128)(2,1)S(1)} fusion(bf16[2048,8,128]{0,2,1:T(8,128)(2,1)} %get-tuple-element.283, f32[8,128,4,2048]{3,1,2,0:T(8,128)} %get-tuple-element.232, f32[8,4,128]{2,1,0:T(4,128)S(1)} %get-tuple-element.233, pred[128,2048]{1,0:T(8,128)(4,1)S(1)} %and_and_fusion.2, f32[128,8,4]{0,2,1:T(4,128)S(1)} %bitcast.110), kind=kOutput, calls=%fused_computation.19.clone.1 | convolution fusion | flops 2182086656 | bytes 39092224 | tf_op jit(solution)/shard_map/while/body/eval_jaxpr/jgqk,kjd->qjgd/dot_general | solution.py:45
  198.0 0.9 copy.35
  198.9 1.1 constant_dynamic-update-slice_fusion.2
  200.0 0.3 and_and_fusion.2
  200.3 1.6 constant_dynamic-slice_fusion.4
  201.9 16.3 %bitcast_reduce_fusion.2 = (f32[8,4,128]{2,1,0:T(4,128)S(1)}, f32[8,128,4,2048]{3,1,2,0:T(8,128)}) fusion(pred[128,2048]{1,0:T(8,128)(4,1)S(1)} %and_and_fusion.2, bf16[2048,8,128]{2,0,1:T(8,128)(2,1)} %get-tuple-element.282, bf16[1,128,8,4,128]{4,3,2,1,0:T(4,128)(2,1)S(1)} %constant_dynamic-slice_fusion.4), kind=kOutput, calls=%fused_computation.8.clone.1 | convolution fusion | flops 2172645376 | bytes 39075840 | tf_op jit(solution)/shard_map/while/body/eval_jaxpr/qjgd,kjd->jgqk/dot_general | solution.py:32
  218.2 15.0 %fusion.37 = f32[8,4,128]{2,1,0:T(4,128)S(1)} fusion(f32[8,128,4,2048]{3,1,2,0:T(8,128)} %get-tuple-element.232, f32[8,4,128]{2,1,0:T(4,128)S(1)} %get-tuple-element.233, pred[128,2048]{1,0:T(8,128)(4,1)S(1)} %and_and_fusion.2), kind=kLoop, calls=%fused_computation.11.clone.1 | loop fusion | flops 33550336 | bytes 33849344 | tf_op jit(solution)/shard_map/while/body/eval_jaxpr/reduce_sum | solution.py:44
  233.2 15.9 %fusion.38 = bf16[128,8,4,128]{0,3,2,1:T(8,128)(2,1)S(1)} fusion(bf16[2048,8,128]{0,2,1:T(8,128)(2,1)} %get-tuple-element.283, f32[8,128,4,2048]{3,1,2,0:T(8,128)} %get-tuple-element.232, f32[8,4,128]{2,1,0:T(4,128)S(1)} %get-tuple-element.233, pred[128,2048]{1,0:T(8,128)(4,1)S(1)} %and_and_fusion.2, f32[128,8,4]{0,2,1:T(4,128)S(1)} %bitcast.110), kind=kOutput, calls=%fused_computation.19.clone.1 | convolution fusion | flops 2182086656 | bytes 39092224 | tf_op jit(solution)/shard_map/while/body/eval_jaxpr/jgqk,kjd->qjgd/dot_general | solution.py:45
  249.1 0.9 copy.35
  250.0 1.1 constant_dynamic-update-slice_fusion.2
  251.1 4.2 %reshape_reshape_reshape.7 = bf16[32,8,4096]{2,1,0:T(8,128)(2,1)} reshape(bf16[2,128,8,512]{3,2,1,0:T(8,128)(2,1)} %get-tuple-element.80) | data formatting | bytes 4194304 | tf_op jit(solution)/shard_map/reshape;reshape;reshape | solution.py:155
  255.3 5.6 %all-to-all-start.4 = ((bf16[32,8,4096]{2,1,0:T(8,128)(2,1)}), bf16[32,8,4096]{2,1,0:T(8,128)(2,1)S(1)}, u32[]{:S(2)}, u32[]{:S(2)}) async-start(bf16[32,8,4096]{2,1,0:T(8,128)(2,1)} %reshape_reshape_reshape.7), calls=%async_computation.4 | async-start | bytes 4194304 | tf_op jit(solution)/shard_map/all_to_all | solution.py:154
  260.9 47.5 %all-to-all-done.4 = bf16[32,8,4096]{2,1,0:T(8,128)(2,1)S(1)} async-done(((bf16[32,8,4096]{2,1,0:T(8,128)(2,1)}), bf16[32,8,4096]{2,1,0:T(8,128)(2,1)S(1)}, u32[]{:S(2)}, u32[]{:S(2)}) %all-to-all-start.4) | async-done | bytes 2097184 | tf_op jit(solution)/shard_map/all_to_all | solution.py:154
  308.4 2.2 gather_fusion
  (71 shorter events, 4.4 us)
Async XLA Ops:
  6.5 64.7 %copy-start.2 = (s32[1,2]{1,0:T(1,128)S(1)}, s32[1,2]{1,0:T(1,128)}, u32[]{:S(2)}) copy-start(s32[1,2]{1,0:T(1,128)} %param.13) | copy-start | bytes 28
  6.5 130.9 %all-gather.4.cloned.1.call-start = ((), (), s32[]{:S(2)}) async-start(), calls=%async_computation.5 | async-start | bytes 4718592 | tf_op jit(solution)/shard_map/all_gather | solution.py:138
  9.0 66.9 %copy-start = (s32[128]{0:T(128)}, s32[128]{0:T(128)S(1)}, u32[]{:S(2)}) copy-start(s32[128]{0:T(128)S(1)} %fusion.26) | copy-start | bytes 1540
  39.9 102.3 %all-gather.6.cloned.1.call-start = ((), (), s32[]{:S(2)}) async-start(), calls=%async_computation.6 | async-start | bytes 4718592 | tf_op jit(solution)/shard_map/all_gather | solution.py:139
  65.7 14.1 %all-to-all-start = ((s32[32,1,8]{2,1,0:T(1,128)}), s32[32,1,8]{2,1,0:T(1,128)S(1)}, u32[]{:S(2)}, u32[]{:S(2)}) async-start(s32[32,1,8]{2,1,0:T(1,128)} %bitcast.17), calls=%async_computation | async-start | bytes 32768 | tf_op jit(solution)/shard_map/all_to_all | solution.py:127
  79.8 55.0 %all-to-all-start.1 = ((bf16[32,8,4096]{2,1,0:T(8,128)(2,1)}), bf16[32,8,4096]{2,1,0:T(8,128)(2,1)S(1)}, u32[]{:S(2)}, u32[]{:S(2)}) async-start(bf16[32,8,4096]{2,1,0:T(8,128)(2,1)} %bitcast.22), calls=%async_computation.1 | async-start | bytes 4194304 | tf_op jit(solution)/shard_map/all_to_all | solution.py:106
  251.1 9.8 %copy-start.1 = (s32[128]{0:T(128)S(1)}, s32[128]{0:T(128)}, u32[]{:S(2)}) copy-start(s32[128]{0:T(128)} %copy-done) | copy-start | bytes 1540
  255.3 53.1 %all-to-all-start.4 = ((bf16[32,8,4096]{2,1,0:T(8,128)(2,1)}), bf16[32,8,4096]{2,1,0:T(8,128)(2,1)S(1)}, u32[]{:S(2)}, u32[]{:S(2)}) async-start(bf16[32,8,4096]{2,1,0:T(8,128)(2,1)} %reshape_reshape_reshape.7), calls=%async_computation.4 | async-start | bytes 4194304 | tf_op jit(solution)/shard_map/all_to_all | solution.py:154
Sparse Core Ops, SparseCore 0:
  40.1 31.3 all-gather.3
  73.3 34.5 all-gather.5
where the time goes:
time: 319 us; the launch traced here: 317 us
  waiting for transfers between devices  82.5 us (26%)
  matrix products  64.3 us (20%)
  blocking collectives  60.7 us (19%)
  local copies, waits for them, and re-layouts  40.5 us (13%)
  other arithmetic  38.6 us (12%)
  starting transfers between devices  17 us (5%)
  between operations  13.5 us (4%)
    all_to_all x1, waiting for transfers between devices, body(): lax.all_to_all(back_rows.reshape(dp_count, slot_rows, back_rows.shape[1])...  47.5 us
    dot_general x2, matrix products, attend(): jnp.einsum('qjgd,kjd->jgqk', block_of_queries, key_heads, preferred_eleme...  32.5 us
    dot_general x2, matrix products, attend(): jnp.einsum('jgqk,kjd->qjgd', weights.astype(jnp.bfloat16), value_heads, p...  31.8 us
    all_to_all x1, waiting for transfers between devices, body(): lax.all_to_all(send_query.reshape(dp_count, slot_rows, query_rows.shape[1...  30.9 us
    reduce_sum x2, other arithmetic, attend(): totals = jnp.sum(weights, axis=3)  30 us
    all_to_all x1, blocking collectives, body(): lax.all_to_all(send_key.reshape(dp_count, slot_rows, key_rows.shape[1]),...  28.3 us
    all_to_all x1, blocking collectives, body(): lax.all_to_all(send_value.reshape(dp_count, slot_rows, token_values.shape...  21.3 us
    while x2, local copies, waits for them, and re-layouts, attend_all(): result = lax.map(one_block, shaped)  11.5 us
  transfers between devices with their start and end apart: 5, of which 3 were waited for; matrix products, arithmetic and copies ran while one was open for 7% of the time, Pallas kernels for 0%

commit v1 on v0

--- a/solution.py
+++ b/solution.py
@@ -8,6 +8,11 @@
 KEY_VALUE_HEADS = 8
 HEAD_SIZE = 128
 masked_score = -1e30
+
+
+def exchange_gather(x, mesh_axis, along):
+    sent = jnp.stack([x] * lax.axis_size(mesh_axis))
+    return jnp.concatenate(lax.all_to_all(sent, mesh_axis, 0, 0), axis=along)
 
 
 def rank_rows(indices):
@@ -137,7 +142,7 @@
     group_key, group_value, group_index = (
         lax.all_gather(local_key, "ctx", axis=0, tiled=True),
         lax.all_gather(local_value, "ctx", axis=0, tiled=True),
-        lax.all_gather(local_index, "ctx", axis=0, tiled=True),
+        exchange_gather(local_index, "ctx", 0),
     )
     group_doc = document_ids(rank_rows(group_index), starts)
     own_doc = lax.dynamic_slice_in_dim(group_doc, lax.axis_index("ctx") * send_count, send_count, 0)

time: 319 us -> 333 us (1.044)
  waiting for transfers between devices: 82.5 us -> 101 us
  blocking collectives: 60.7 us -> 49.7 us
  starting transfers between devices: 17 us -> 21.9 us
    all_to_all x1, waiting for transfers between devices: 30.9 us -> 43.7 us  [body(): lax.all_to_all(send_query.reshape(dp_count, slot_rows, query_rows.shape[1...]
    all_gather x1 -> x0, blocking collectives: 11 us -> none  [body(): lax.all_gather(local_index, 'ctx', axis=0, tiled=True)]
    all_to_all x1, waiting for transfers between devices: 3.97 us -> 8.36 us  [body(): lax.all_to_all(send_index.reshape(dp_count, slot_rows), 'dp', split_axis=...]
    all_to_all x0 -> x1, starting transfers between devices: none -> 4.3 us  [exchange_gather(): return jnp.concatenate(lax.all_to_all(sent, mesh_axis, 0, 0), axis=along)]
  transfers between devices with their start and end apart: 5 -> 6, of which waited for: 3 -> 4; matrix products, arithmetic and copies ran while one was open for 7% -> 7% of each run, Pallas kernels for 0% -> 0%
where the time goes in v1:
time: 333 us; the launch traced here: 331 us
  waiting for transfers between devices  101 us (30%)
  matrix products  64.3 us (19%)
  blocking collectives  49.7 us (15%)
  local copies, waits for them, and re-layouts  41.3 us (12%)
  other arithmetic  38.6 us (12%)
  starting transfers between devices  21.9 us (7%)
  between operations  13.6 us (4%)
    all_to_all x1, waiting for transfers between devices, body(): lax.all_to_all(back_rows.reshape(dp_count, slot_rows, back_rows.shape[1])...  48.6 us
    all_to_all x1, waiting for transfers between devices, body(): lax.all_to_all(send_query.reshape(dp_count, slot_rows, query_rows.shape[1...  43.7 us
    dot_general x2, matrix products, attend(): jnp.einsum('qjgd,kjd->jgqk', block_of_queries, key_heads, preferred_eleme...  32.5 us
    dot_general x2, matrix products, attend(): jnp.einsum('jgqk,kjd->qjgd', weights.astype(jnp.bfloat16), value_heads, p...  31.8 us
    reduce_sum x2, other arithmetic, attend(): totals = jnp.sum(weights, axis=3)  30 us
    all_to_all x1, blocking collectives, body(): lax.all_to_all(send_key.reshape(dp_count, slot_rows, key_rows.shape[1]),...  28.3 us
    all_to_all x1, blocking collectives, body(): lax.all_to_all(send_value.reshape(dp_count, slot_rows, token_values.shape...  21.3 us
    while x2, local copies, waits for them, and re-layouts, attend_all(): result = lax.map(one_block, shaped)  11.5 us
  transfers between devices with their start and end apart: 6, of which 4 were waited for; matrix products, arithmetic and copies ran while one was open for 7% of the time, Pallas kernels for 0%

profile of v1, /device:TPU:8, one launch (start us, length us, event | category | flops | bytes accessed | tf_op | source)
XLA Modules:
  0.0 331.4 jit_solution(15419932694990189748)
XLA Ops:
  6.5 0.7 fusion.24
  7.5 0.8 select_reduce_fusion
  8.3 0.7 fusion.26
  9.0 1.7 scatter_custom_fusion.2
  10.7 28.3 %all_to_all.38 = bf16[32,8,1024]{2,1,0:T(8,128)(2,1)S(1)} all-to-all(bf16[32,8,1024]{2,1,0:T(8,128)(2,1)S(1)} %bitcast.116), channel_id=1, replica_groups=mesh['dp'=32,'ctx'=8] {'dp'}, dimensions={0} | all-to-all | bytes 1048576 | tf_op jit(solution)/shard_map/all_to_all | solution.py:118
  39.0 0.9 copy.33
  40.0 1.7 scatter_custom_fusion.3
  41.7 21.3 %all_to_all.39 = bf16[32,8,1024]{2,1,0:T(8,128)(2,1)S(1)} all-to-all(bf16[32,8,1024]{2,1,0:T(8,128)(2,1)S(1)} %bitcast.117), channel_id=1, replica_groups=mesh['dp'=32,'ctx'=8] {'dp'}, dimensions={0} | all-to-all | bytes 1048576 | tf_op jit(solution)/shard_map/all_to_all | solution.py:125
  63.1 0.9 copy.34
  64.0 1.0 scatter_custom_fusion
  65.0 0.7 all_to_all.24
  65.7 5.6 %all-to-all-start = ((s32[32,1,8]{2,1,0:T(1,128)}), s32[32,1,8]{2,1,0:T(1,128)S(1)}, u32[]{:S(2)}, u32[]{:S(2)}) async-start(s32[32,1,8]{2,1,0:T(1,128)} %bitcast.17), calls=%async_computation | async-start | bytes 32768 | tf_op jit(solution)/shard_map/all_to_all | solution.py:132
  71.4 8.4 %all-to-all-done = s32[32,1,8]{2,1,0:T(1,128)S(1)} async-done(((s32[32,1,8]{2,1,0:T(1,128)}), s32[32,1,8]{2,1,0:T(1,128)S(1)}, u32[]{:S(2)}, u32[]{:S(2)}) %all-to-all-start) | async-done | bytes 1056 | tf_op jit(solution)/shard_map/all_to_all | solution.py:132
  79.8 0.5 broadcast.121
  80.3 0.7 reduce.7
  81.1 0.6 stack.6
  81.7 4.3 %all-to-all-start.1 = ((s32[8,1,256]{2,1,0:T(1,128)}), s32[8,1,256]{2,1,0:T(1,128)S(1)}, u32[]{:S(2)}, u32[]{:S(2)}) async-start(s32[8,1,256]{2,1,0:T(1,128)} %stack.6), calls=%async_computation.1 | async-start | bytes 16384 | tf_op jit(solution)/shard_map/all_to_all | solution.py:15
  86.0 4.5 %scatter_custom_fusion.1 = bf16[256,4096]{1,0:T(8,128)(2,1)} fusion(s32[128]{0:T(128)S(1)} %fusion.26, bf16[128,4096]{1,0:T(8,128)(2,1)} %param.9, bf16[]{:T(256)} %constant.33.clone.1), kind=kCustom, calls=%fused_computation.31 | custom fusion | bytes 2097664 | tf_op jit(solution)/shard_map/scatter | solution.py:103
  90.6 0.8 all-to-all-done.1
  91.4 5.1 %all-to-all-start.2 = ((bf16[32,8,4096]{2,1,0:T(8,128)(2,1)}), bf16[32,8,4096]{2,1,0:T(8,128)(2,1)S(1)}, u32[]{:S(2)}, u32[]{:S(2)}) async-start(bf16[32,8,4096]{2,1,0:T(8,128)(2,1)} %bitcast.21), calls=%async_computation.2 | async-start | bytes 4194304 | tf_op jit(solution)/shard_map/all_to_all | solution.py:111
  96.6 5.8 %while.20 = (s32[]{:T(128)}, s32[16,128]{1,0:T(8,128)S(1)}, pred[2048]{0:T(1024)(128)(4,1)S(1)}, s32[8,256]{1,0:T(8,128)S(1)}, s32[16,128]{1,0:T(8,128)S(1)}, /*index=5*/s32[]{:T(128)}, s32[]{:T(128)}) while((s32[]{:T(128)}, s32[16,128]{1,0:T(8,128)S(1)}, pred[2048]{0:T(1024)(128)(4,1)S(1)}, s32[8,256]{1,0:T(8,128)S(1)}, ...), condition=%wide.region_7.8_spmd, body=%wide.region_5.7_spmd.sunk | while | flops 1048450 | bytes 29781 | solution.py:27
  97.0 0.3 convert_reduce_fusion.2
  98.5 0.3 convert_reduce_fusion.2
  100.3 0.3 convert_reduce_fusion.2
  102.1 0.3 convert_reduce_fusion.2
  102.6 43.7 %all-to-all-done.2 = bf16[32,8,4096]{2,1,0:T(8,128)(2,1)S(1)} async-done(((bf16[32,8,4096]{2,1,0:T(8,128)(2,1)}), bf16[32,8,4096]{2,1,0:T(8,128)(2,1)S(1)}, u32[]{:S(2)}, u32[]{:S(2)}) %all-to-all-start.2) | async-done | bytes 2097184 | tf_op jit(solution)/shard_map/all_to_all | solution.py:111
  146.3 2.7 reshape_reshape_reshape.6
  149.0 4.8 %copy.22 = bf16[2048,8,128]{2,0,1:T(8,128)(2,1)} copy(bf16[2048,8,128]{2,1,0:T(8,128)(2,1)} %all-gather.3.cloned.1.call-done) | data formatting | bytes 8388608 | tf_op jit(solution)/shard_map/while | solution.py:83
  153.7 6.7 %copy.23 = bf16[2048,8,128]{0,2,1:T(8,128)(2,1)} copy(bf16[2048,8,128]{2,1,0:T(8,128)(2,1)} %all-gather.5.cloned.1.call-done) | data formatting | bytes 8388608 | tf_op jit(solution)/shard_map/while | solution.py:83
  160.4 102.2 %while.21 = (s32[]{:T(128)}, bf16[2,128,8,512]{3,2,1,0:T(8,128)(2,1)}, s32[2,128]{1,0:T(2,128)S(1)}, s32[2048]{0:T(1024)S(1)}, s32[8,256]{1,0:T(8,128)S(1)}, /*i...) while((s32[]{:T(128)}, ...), condition=%wide.region_14.15_spmd, body=%wide.region_11.14_spmd.sunk | while | flops 4389332992 | bytes 118619752 | solution.py:83
  160.4 0.3 and_and_fusion.2
  160.8 1.6 constant_dynamic-slice_fusion.4
  162.4 16.3 %bitcast_reduce_fusion.2 = (f32[8,4,128]{2,1,0:T(4,128)S(1)}, f32[8,128,4,2048]{3,1,2,0:T(8,128)}) fusion(pred[128,2048]{1,0:T(8,128)(4,1)S(1)} %and_and_fusion.2, bf16[2048,8,128]{2,0,1:T(8,128)(2,1)} %get-tuple-element.291, bf16[1,128,8,4,128]{4,3,2,1,0:T(4,128)(2,1)S(1)} %constant_dynamic-slice_fusion.4), kind=kOutput, calls=%fused_computation.8.clone.1 | convolution fusion | flops 2172645376 | bytes 39075840 | tf_op jit(solution)/shard_map/while/body/eval_jaxpr/qjgd,kjd->jgqk/dot_general | solution.py:37
  178.6 15.0 %fusion.37 = f32[8,4,128]{2,1,0:T(4,128)S(1)} fusion(f32[8,128,4,2048]{3,1,2,0:T(8,128)} %get-tuple-element.241, f32[8,4,128]{2,1,0:T(4,128)S(1)} %get-tuple-element.242, pred[128,2048]{1,0:T(8,128)(4,1)S(1)} %and_and_fusion.2), kind=kLoop, calls=%fused_computation.11.clone.1 | loop fusion | flops 33550336 | bytes 33849344 | tf_op jit(solution)/shard_map/while/body/eval_jaxpr/reduce_sum | solution.py:49
  193.6 15.9 %fusion.38 = bf16[128,8,4,128]{0,3,2,1:T(8,128)(2,1)S(1)} fusion(bf16[2048,8,128]{0,2,1:T(8,128)(2,1)} %get-tuple-element.292, f32[8,128,4,2048]{3,1,2,0:T(8,128)} %get-tuple-element.241, f32[8,4,128]{2,1,0:T(4,128)S(1)} %get-tuple-element.242, pred[128,2048]{1,0:T(8,128)(4,1)S(1)} %and_and_fusion.2, f32[128,8,4]{0,2,1:T(4,128)S(1)} %bitcast.124), kind=kOutput, calls=%fused_computation.19.clone.1 | convolution fusion | flops 2182086656 | bytes 39092224 | tf_op jit(solution)/shard_map/while/body/eval_jaxpr/jgqk,kjd->qjgd/dot_general | solution.py:50
  209.5 0.9 copy.48
  210.4 1.1 constant_dynamic-update-slice_fusion.2
  211.5 0.3 and_and_fusion.2
  211.9 1.6 constant_dynamic-slice_fusion.4
  213.5 16.3 %bitcast_reduce_fusion.2 = (f32[8,4,128]{2,1,0:T(4,128)S(1)}, f32[8,128,4,2048]{3,1,2,0:T(8,128)}) fusion(pred[128,2048]{1,0:T(8,128)(4,1)S(1)} %and_and_fusion.2, bf16[2048,8,128]{2,0,1:T(8,128)(2,1)} %get-tuple-element.291, bf16[1,128,8,4,128]{4,3,2,1,0:T(4,128)(2,1)S(1)} %constant_dynamic-slice_fusion.4), kind=kOutput, calls=%fused_computation.8.clone.1 | convolution fusion | flops 2172645376 | bytes 39075840 | tf_op jit(solution)/shard_map/while/body/eval_jaxpr/qjgd,kjd->jgqk/dot_general | solution.py:37
  229.7 15.0 %fusion.37 = f32[8,4,128]{2,1,0:T(4,128)S(1)} fusion(f32[8,128,4,2048]{3,1,2,0:T(8,128)} %get-tuple-element.241, f32[8,4,128]{2,1,0:T(4,128)S(1)} %get-tuple-element.242, pred[128,2048]{1,0:T(8,128)(4,1)S(1)} %and_and_fusion.2), kind=kLoop, calls=%fused_computation.11.clone.1 | loop fusion | flops 33550336 | bytes 33849344 | tf_op jit(solution)/shard_map/while/body/eval_jaxpr/reduce_sum | solution.py:49
  244.7 15.9 %fusion.38 = bf16[128,8,4,128]{0,3,2,1:T(8,128)(2,1)S(1)} fusion(bf16[2048,8,128]{0,2,1:T(8,128)(2,1)} %get-tuple-element.292, f32[8,128,4,2048]{3,1,2,0:T(8,128)} %get-tuple-element.241, f32[8,4,128]{2,1,0:T(4,128)S(1)} %get-tuple-element.242, pred[128,2048]{1,0:T(8,128)(4,1)S(1)} %and_and_fusion.2, f32[128,8,4]{0,2,1:T(4,128)S(1)} %bitcast.124), kind=kOutput, calls=%fused_computation.19.clone.1 | convolution fusion | flops 2182086656 | bytes 39092224 | tf_op jit(solution)/shard_map/while/body/eval_jaxpr/jgqk,kjd->qjgd/dot_general | solution.py:50
  260.6 0.9 copy.48
  261.5 1.1 constant_dynamic-update-slice_fusion.2
  262.6 4.2 %reshape_reshape_reshape.7 = bf16[32,8,4096]{2,1,0:T(8,128)(2,1)} reshape(bf16[2,128,8,512]{3,2,1,0:T(8,128)(2,1)} %get-tuple-element.80) | data formatting | bytes 4194304 | tf_op jit(solution)/shard_map/reshape;reshape;reshape | solution.py:160
  266.8 6.9 %all-to-all-start.5 = ((bf16[32,8,4096]{2,1,0:T(8,128)(2,1)}), bf16[32,8,4096]{2,1,0:T(8,128)(2,1)S(1)}, u32[]{:S(2)}, u32[]{:S(2)}) async-start(bf16[32,8,4096]{2,1,0:T(8,128)(2,1)} %reshape_reshape_reshape.7), calls=%async_computation.5 | async-start | bytes 4194304 | tf_op jit(solution)/shard_map/all_to_all | solution.py:159
  273.7 48.6 %all-to-all-done.5 = bf16[32,8,4096]{2,1,0:T(8,128)(2,1)S(1)} async-done(((bf16[32,8,4096]{2,1,0:T(8,128)(2,1)}), bf16[32,8,4096]{2,1,0:T(8,128)(2,1)S(1)}, u32[]{:S(2)}, u32[]{:S(2)}) %all-to-all-start.5) | async-done | bytes 2097184 | tf_op jit(solution)/shard_map/all_to_all | solution.py:159
  322.4 2.2 gather_fusion
  (93 shorter events, 5.1 us)
Async XLA Ops:
  6.5 64.7 %copy-start.2 = (s32[1,2]{1,0:T(1,128)S(1)}, s32[1,2]{1,0:T(1,128)}, u32[]{:S(2)}) copy-start(s32[1,2]{1,0:T(1,128)} %param.13) | copy-start | bytes 28
  6.5 142.4 %all-gather.3.cloned.1.call-start = ((), (), s32[]{:S(2)}) async-start(), calls=%async_computation.6 | async-start | bytes 4718592 | tf_op jit(solution)/shard_map/all_gather | solution.py:143
  9.0 81.6 %copy-start = (s32[128]{0:T(128)}, s32[128]{0:T(128)S(1)}, u32[]{:S(2)}) copy-start(s32[128]{0:T(128)S(1)} %fusion.26) | copy-start | bytes 1540
  39.9 113.8 %all-gather.5.cloned.1.call-start = ((), (), s32[]{:S(2)}) async-start(), calls=%async_computation.7 | async-start | bytes 4718592 | tf_op jit(solution)/shard_map/all_gather | solution.py:144
  65.7 14.1 %all-to-all-start = ((s32[32,1,8]{2,1,0:T(1,128)}), s32[32,1,8]{2,1,0:T(1,128)S(1)}, u32[]{:S(2)}, u32[]{:S(2)}) async-start(s32[32,1,8]{2,1,0:T(1,128)} %bitcast.17), calls=%async_computation | async-start | bytes 32768 | tf_op jit(solution)/shard_map/all_to_all | solution.py:132
  81.7 9.7 %all-to-all-start.1 = ((s32[8,1,256]{2,1,0:T(1,128)}), s32[8,1,256]{2,1,0:T(1,128)S(1)}, u32[]{:S(2)}, u32[]{:S(2)}) async-start(s32[8,1,256]{2,1,0:T(1,128)} %stack.6), calls=%async_computation.1 | async-start | bytes 16384 | tf_op jit(solution)/shard_map/all_to_all | solution.py:15
  91.4 54.9 %all-to-all-start.2 = ((bf16[32,8,4096]{2,1,0:T(8,128)(2,1)}), bf16[32,8,4096]{2,1,0:T(8,128)(2,1)S(1)}, u32[]{:S(2)}, u32[]{:S(2)}) async-start(bf16[32,8,4096]{2,1,0:T(8,128)(2,1)} %bitcast.21), calls=%async_computation.2 | async-start | bytes 4194304 | tf_op jit(solution)/shard_map/all_to_all | solution.py:111
  262.6 11.1 %copy-start.1 = (s32[128]{0:T(128)S(1)}, s32[128]{0:T(128)}, u32[]{:S(2)}) copy-start(s32[128]{0:T(128)} %copy-done) | copy-start | bytes 1540
  266.8 55.5 %all-to-all-start.5 = ((bf16[32,8,4096]{2,1,0:T(8,128)(2,1)}), bf16[32,8,4096]{2,1,0:T(8,128)(2,1)S(1)}, u32[]{:S(2)}, u32[]{:S(2)}) async-start(bf16[32,8,4096]{2,1,0:T(8,128)(2,1)} %reshape_reshape_reshape.7), calls=%async_computation.5 | async-start | bytes 4194304 | tf_op jit(solution)/shard_map/all_to_all | solution.py:159
Sparse Core Ops, SparseCore 0:
  40.1 31.3 all-gather.2
  73.3 34.6 all-gather.4
